TPU v7x, 256 devices: a whole 4x4x8 slice. The times are simulated.
256 devices in a mesh: blk: 64 (over y_lo, z, x), rep: 4 (over y_hi, core).
Axes of the slice: x: 4, y: 4 (y_hi: 2, y_lo: 2; y = y_hi * 2 + y_lo), z: 8, core: 2. Of those that a mesh axis runs over, the one named last changes fastest.
Arguments:
- points: bfloat16 [49152, 1024], P('blk'), may hold values from -6 to 6
- w_in: bfloat16 [1024, 512], replicated, may hold values from -0.1875 to 0.1875
- b_in: float32 [512], replicated, may hold values from -3 to 3
- w_out: bfloat16 [512, 64], replicated, may hold values from -0.25 to 0.25
- inv_scale: float32 [64], replicated, may hold values from 0.05 to 0.5
- solves: bfloat16 [64, 49152], P(None, 'blk'), may hold values from -1 to 1
- probes: bfloat16 [64, 49152], P(None, 'blk'), may hold values from -1 to 1
Outputs:
- feat_grad: float32 [64, 49152], P(None, ('blk', 'rep'))
- grad_w_in: float32 [1024, 512], replicated
- grad_b_in: float32 [512], replicated
- grad_w_out: float32 [512, 64], replicated
All inputs are finite; a program needn't handle non-finite values.
Results may differ from a plain program's by a relative error of at most 0.034.
Values may be sent and summed in bfloat16 or wider, within the bound.
A program may use at most 64 MiB of HBM per device.

v0:
```python
import math
import jax
import jax.numpy as jnp
from jax import lax
from jax.sharding import PartitionSpec as P


def shifted(block, axis, distance):
    devices = range(lax.axis_size(axis))
    route = [((i - distance) % len(devices), i) for i in devices]
    return lax.ppermute(block, axis, route)


def cut_along(value, dim, count):
    lengths = value.shape
    blocks = value.reshape(*lengths[:dim], count, lengths[dim] // count, *lengths[dim + 1 :])
    return jnp.moveaxis(blocks, dim, 0)


def sum_at_owner(value, axis, dim):
    count = lax.axis_size(axis)
    blocks = lax.all_to_all(cut_along(value, dim, count), axis, 0, 0, tiled=True)
    return jnp.sum(blocks, axis=0)


def couple(own_y, own_pair, own_sq, visitor, feat):
    vis_y = visitor[:feat]
    vis_pair = visitor[feat:]
    vis_sq = jnp.sum(jnp.square(vis_y.astype(jnp.float32)), axis=0)
    cross = lax.dot_general(
        own_y, vis_y, (((0,), (0,)), ((), ())), preferred_element_type=jnp.float32
    )
    kernel = jnp.exp(-0.5 * (own_sq[:, None] + vis_sq[None, :] - 2.0 * cross))
    coupling = lax.dot_general(
        own_pair, vis_pair, (((0,), (0,)), ((), ())), preferred_element_type=jnp.float32
    )
    weight_b = (coupling * kernel).astype(jnp.bfloat16)
    totals = jnp.sum(weight_b.astype(jnp.float32), axis=1)
    pull = lax.dot_general(
        vis_y, weight_b, (((1,), (1,)), ((), ())), preferred_element_type=jnp.float32
    )
    return (totals, pull)


def on_device(points, w_in, b_in, w_out, inv_scale, solves, probes):
    feat = w_out.shape[1]
    reps = lax.axis_size("rep")
    blocks = lax.axis_size("blk")
    rep_index = lax.axis_index("rep")
    rows = points.shape[0]
    quarter = rows // reps
    first = rep_index * quarter
    npts = rows * blocks
    levels = reps.bit_length() - 1
    own_points = lax.dynamic_slice_in_dim(points, first, quarter, 0)
    hidden = jnp.tanh(jnp.dot(points, w_in, preferred_element_type=jnp.float32) + b_in).astype(
        jnp.bfloat16
    )
    pre = lax.dot_general(
        w_out, hidden, (((0,), (1,)), ((), ())), preferred_element_type=jnp.float32
    )
    hidden, scaled = (hidden, (pre * inv_scale[:, None]).astype(jnp.bfloat16))
    own_hidden = lax.dynamic_slice_in_dim(hidden, first, quarter, 0)
    own_pair = jnp.concatenate([solves, probes], axis=0)
    own_sq = jnp.sum(jnp.square(scaled.astype(jnp.float32)), axis=0)
    scaled32 = scaled.astype(jnp.float32)
    visitor = jnp.concatenate([scaled, probes, solves], axis=0)
    for bit in range(levels):
        moved = shifted(visitor, "blk", -(1 << bit))
        visitor = jnp.where(rep_index // (1 << bit) % 2 == 1, moved, visitor)

    def accumulate(state, vis):
        totals, pull = couple(scaled, own_pair, own_sq, vis, feat)
        return (state[0] + totals, state[1] + pull)

    init = (jnp.zeros((rows,), jnp.float32), jnp.zeros((feat, rows), jnp.float32))
    steps = blocks // reps
    behind = shifted(visitor, "blk", reps)

    def advance_both(index, carry):
        state, ahead_vis, behind_vis = carry
        state = accumulate(accumulate(state, ahead_vis), behind_vis)
        ahead_vis = shifted(ahead_vis, "blk", -reps)
        behind_vis = shifted(behind_vis, "blk", reps)
        return (state, ahead_vis, behind_vis)

    state, ahead_vis, behind_vis = lax.fori_loop(
        0, steps // 2 - 1, advance_both, (init, visitor, behind)
    )
    state = accumulate(accumulate(state, ahead_vis), behind_vis)
    totals, pull = state
    drift = pull - scaled32 * totals[None, :]
    summed = sum_at_owner(drift, "rep", 1)
    feat_grad = summed * inv_scale[:, None]
    grad_b16 = feat_grad.astype(jnp.bfloat16)
    back = lax.dot_general(
        grad_b16, w_out, (((0,), (1,)), ((), ())), preferred_element_type=jnp.float32
    )
    hid32 = own_hidden.astype(jnp.float32)
    pre_grad = back * (1.0 - hid32 * hid32)
    norm = 1.0 / math.sqrt(npts)
    term_w_in = (
        lax.dot_general(
            own_points,
            pre_grad.astype(jnp.bfloat16),
            (((0,), (0,)), ((), ())),
            preferred_element_type=jnp.float32,
        )
        * norm
    )
    term_b_in = jnp.sum(pre_grad, axis=0) * norm
    term_w_out = (
        lax.dot_general(
            own_hidden, grad_b16, (((0,), (1,)), ((), ())), preferred_element_type=jnp.float32
        )
        * norm
    )
    grad_w_in, grad_b_in, grad_w_out = lax.psum((term_w_in, term_b_in, term_w_out), ("blk", "rep"))
    return (feat_grad, grad_w_in, grad_b_in, grad_w_out)


def solution(mesh):
    in_specs = (P("blk", None), P(), P(), P(), P(), P(None, "blk"), P(None, "blk"))
    out_specs = (P(None, ("blk", "rep")), P(), P(), P())
    return jax.shard_map(
        on_device, mesh=mesh, in_specs=in_specs, out_specs=out_specs, check_vma=False
    )
```

profile of v0, /device:TPU:2, one launch (start us, length us, event | category | flops | bytes accessed | tf_op | source)
XLA Modules:
  0.0 443.5 jit_solution(13951835075255544906)
XLA Ops:
  8.6 2.2 tanh_convert_fusion
  13.6 2.3 collective-permute-start.2
  16.0 6.5 %collective-permute-done.2 = bf16[192,768]{1,0:T(8,128)(2,1)S(1)} collective-permute-done((bf16[192,768]{1,0:T(8,128)(2,1)S(1)}, bf16[192,768]{1,0:T(8,128)(2,1)S(1)}, u32[]{:S(2)}, u32[]{:S(2)}) %collective-permute-start.2) | collective-permute-done | bytes 294944 | tf_op jit(solution)/shard_map/ppermute | solution.py:11
  23.4 12.7 %collective-permute-start.3 = (bf16[192,768]{1,0:T(8,128)(2,1)S(1)}, bf16[192,768]{1,0:T(8,128)(2,1)S(1)}, u32[]{:S(2)}, u32[]{:S(2)}) collective-permute-start(bf16[192,768]{1,0:T(8,128)(2,1)S(1)} %broadcast_select_fusion), channel_id=1, source_target_pairs={{8,0},{12,4},{16,8},{20,12},{24,16},{28,20},{32,24},{36,28},{40,32... | collective-permute-start | bytes 884744 | tf_op jit(solution)/shard_map/ppermute | solution.py:11
  36.2 5.4 %collective-permute-done.3 = bf16[192,768]{1,0:T(8,128)(2,1)S(1)} collective-permute-done((bf16[192,768]{1,0:T(8,128)(2,1)S(1)}, bf16[192,768]{1,0:T(8,128)(2,1)S(1)}, u32[]{:S(2)}, u32[]{:S(2)}) %collective-permute-start.3) | collective-permute-done | bytes 294944 | tf_op jit(solution)/shard_map/ppermute | solution.py:11
  42.3 9.3 %collective-permute-done.4 = bf16[192,768]{1,0:T(8,128)(2,1)} collective-permute-done((bf16[192,768]{1,0:T(8,128)(2,1)}, bf16[192,768]{1,0:T(8,128)(2,1)}, u32[]{:S(2)}, u32[]{:S(2)}) %collective-permute-start.4) | collective-permute-done | bytes 294944 | tf_op jit(solution)/shard_map/ppermute | solution.py:11
  51.7 93.9 %while.17 = (s32[]{:T(128)}, f32[768]{0:T(1024)S(1)}, f32[64,768]{1,0:T(8,128)}, bf16[192,768]{1,0:T(8,128)(2,1)}, bf16[192,768]{1,0:T(8,128)(2,1)}, /*index=5*/...) while((s32[]{:T(128)}, f32[768]{0:T(1024)S(1)}, ...), condition=%wide.region_6.7_spmd.clone, body=%wide.region_1.6_spmd.clone.sunk | while | flops 613858560 | bytes 20095168 | solution.py:87
  64.3 2.1 collective-permute-start
  73.1 2.0 fusion.79
  77.3 3.0 collective-permute-start
  86.9 2.0 fusion.79
  91.1 3.0 collective-permute-start
  100.8 2.0 fusion.79
  104.9 3.0 collective-permute-start
  114.6 2.0 fusion.79
  118.8 3.0 collective-permute-start
  128.5 2.0 fusion.79
  132.6 3.0 collective-permute-start
  142.3 2.0 fusion.79
  156.8 4.1 all-to-all-start
  160.9 7.5 %all-to-all-done = f32[4,64,192]{2,1,0:T(8,128)S(1)} async-done(((f32[4,64,192]{2,1,0:T(8,128)}), f32[4,64,192]{2,1,0:T(8,128)S(1)}, u32[]{:S(2)}, u32[]{:S(2)}) %all-to-all-start) | async-done | bytes 196640 | tf_op jit(solution)/shard_map/all_to_all | solution.py:22
  171.5 78.0 %psum.22 = f32[512]{0:T(512)} all-reduce(f32[512]{0:T(512)S(1)} %broadcast_multiply_fusion.1), channel_id=1, replica_groups=mesh['blk'=64,'rep'=4] {'blk','rep'}, use_global_device_ids=true, to_apply=%region_14.15 | all-reduce | flops 512 | bytes 4096 | tf_op jit(solution)/shard_map/psum | solution.py:118
  249.5 183.4 %all-reduce.3.cloned.1.call-done = (f32[1024,512]{1,0:T(8,128)}, f32[512,64]{0,1:T(8,128)}) async-done(((f32[1024,512]{1,0:T(8,128)}, f32[512,64]{0,1:T(8,128)}), (f32[1024,512]{1,0:T(8,128)}, f32[512,64]{0,1:T(8,128)})) %all-reduce.3.cloned.1.call-update) | async-done | bytes 2228240 | tf_op jit(solution)/shard_map/psum | solution.py:118
  432.9 3.1 copy.32
  (138 shorter events, 84.9 us)
Async XLA Ops:
  7.2 4.5 %copy-start.8 = (bf16[512,64]{0,1:T(8,128)(2,1)S(1)}, bf16[512,64]{0,1:T(8,128)(2,1)}, u32[]{:S(2)}) copy-start(bf16[512,64]{0,1:T(8,128)(2,1)} %param.12) | copy-start | bytes 196612
  7.2 5.5 %copy-start.4 = (bf16[64,768]{1,0:T(8,128)(2,1)S(1)}, bf16[64,768]{1,0:T(8,128)(2,1)}, u32[]{:S(2)}) copy-start(bf16[64,768]{1,0:T(8,128)(2,1)} %param.14) | copy-start | bytes 294916
  13.6 8.8 %collective-permute-start.2 = (bf16[192,768]{1,0:T(8,128)(2,1)S(1)}, bf16[192,768]{1,0:T(8,128)(2,1)S(1)}, u32[]{:S(2)}, u32[]{:S(2)}) collective-permute-start(bf16[192,768]{1,0:T(8,128)(2,1)S(1)} %pad_maximum_fusion), channel_id=1, source_target_pairs={{4,0},{8,4},{12,8},{16,12},{20,16},{24,20},{28,24},{32,28},{36,32}... | collective-permute-start | bytes 884744 | tf_op jit(solution)/shard_map/ppermute | solution.py:11
  23.4 18.1 %collective-permute-start.3 = (bf16[192,768]{1,0:T(8,128)(2,1)S(1)}, bf16[192,768]{1,0:T(8,128)(2,1)S(1)}, u32[]{:S(2)}, u32[]{:S(2)}) collective-permute-start(bf16[192,768]{1,0:T(8,128)(2,1)S(1)} %broadcast_select_fusion), channel_id=1, source_target_pairs={{8,0},{12,4},{16,8},{20,12},{24,16},{28,20},{32,24},{36,28},{40,32... | collective-permute-start | bytes 884744 | tf_op jit(solution)/shard_map/ppermute | solution.py:11
  42.3 9.4 %collective-permute-start.4 = (bf16[192,768]{1,0:T(8,128)(2,1)}, bf16[192,768]{1,0:T(8,128)(2,1)}, u32[]{:S(2)}, u32[]{:S(2)}) collective-permute-start(bf16[192,768]{1,0:T(8,128)(2,1)} %broadcast_select_fusion.1), channel_id=1, source_target_pairs={{240,0},{244,4},{248,8},{252,12},{0,16},{4,20},{8,24},{12,28},{16,... | collective-permute-start | bytes 884744 | tf_op jit(solution)/shard_map/ppermute | solution.py:11
  52.6 10.7 %collective-permute-start = (bf16[192,768]{1,0:T(8,128)(2,1)S(1)}, bf16[192,768]{1,0:T(8,128)(2,1)}, u32[]{:S(2)}, u32[]{:S(2)}) collective-permute-start(bf16[192,768]{1,0:T(8,128)(2,1)S(1)} %copy.23), channel_id=1, source_target_pairs={{16,0},{20,4},{24,8},{28,12},{32,16},{36,20},{40,24},{44,28},{48,3... | collective-permute-start | bytes 884744 | tf_op jit(solution)/shard_map/while/body/eval_jaxpr/ppermute | solution.py:11
  53.6 9.7 %collective-permute-start.1 = (bf16[192,768]{1,0:T(8,128)(2,1)S(1)}, bf16[192,768]{1,0:T(8,128)(2,1)}, u32[]{:S(2)}, u32[]{:S(2)}) collective-permute-start(bf16[192,768]{1,0:T(8,128)(2,1)S(1)} %copy.24), channel_id=1, source_target_pairs={{240,0},{244,4},{248,8},{252,12},{0,16},{4,20},{8,24},{12,28},{16,... | collective-permute-start | bytes 884744 | tf_op jit(solution)/shard_map/while/body/eval_jaxpr/ppermute | solution.py:11
  64.3 10.9 %collective-permute-start = (bf16[192,768]{1,0:T(8,128)(2,1)S(1)}, bf16[192,768]{1,0:T(8,128)(2,1)}, u32[]{:S(2)}, u32[]{:S(2)}) collective-permute-start(bf16[192,768]{1,0:T(8,128)(2,1)S(1)} %copy.23), channel_id=1, source_target_pairs={{16,0},{20,4},{24,8},{28,12},{32,16},{36,20},{40,24},{44,28},{48,3... | collective-permute-start | bytes 884744 | tf_op jit(solution)/shard_map/while/body/eval_jaxpr/ppermute | solution.py:11
  67.4 8.9 %collective-permute-start.1 = (bf16[192,768]{1,0:T(8,128)(2,1)S(1)}, bf16[192,768]{1,0:T(8,128)(2,1)}, u32[]{:S(2)}, u32[]{:S(2)}) collective-permute-start(bf16[192,768]{1,0:T(8,128)(2,1)S(1)} %copy.24), channel_id=1, source_target_pairs={{240,0},{244,4},{248,8},{252,12},{0,16},{4,20},{8,24},{12,28},{16,... | collective-permute-start | bytes 884744 | tf_op jit(solution)/shard_map/while/body/eval_jaxpr/ppermute | solution.py:11
  77.3 11.7 %collective-permute-start = (bf16[192,768]{1,0:T(8,128)(2,1)S(1)}, bf16[192,768]{1,0:T(8,128)(2,1)}, u32[]{:S(2)}, u32[]{:S(2)}) collective-permute-start(bf16[192,768]{1,0:T(8,128)(2,1)S(1)} %copy.23), channel_id=1, source_target_pairs={{16,0},{20,4},{24,8},{28,12},{32,16},{36,20},{40,24},{44,28},{48,3... | collective-permute-start | bytes 884744 | tf_op jit(solution)/shard_map/while/body/eval_jaxpr/ppermute | solution.py:11
  81.2 8.9 %collective-permute-start.1 = (bf16[192,768]{1,0:T(8,128)(2,1)S(1)}, bf16[192,768]{1,0:T(8,128)(2,1)}, u32[]{:S(2)}, u32[]{:S(2)}) collective-permute-start(bf16[192,768]{1,0:T(8,128)(2,1)S(1)} %copy.24), channel_id=1, source_target_pairs={{240,0},{244,4},{248,8},{252,12},{0,16},{4,20},{8,24},{12,28},{16,... | collective-permute-start | bytes 884744 | tf_op jit(solution)/shard_map/while/body/eval_jaxpr/ppermute | solution.py:11
  91.1 11.7 %collective-permute-start = (bf16[192,768]{1,0:T(8,128)(2,1)S(1)}, bf16[192,768]{1,0:T(8,128)(2,1)}, u32[]{:S(2)}, u32[]{:S(2)}) collective-permute-start(bf16[192,768]{1,0:T(8,128)(2,1)S(1)} %copy.23), channel_id=1, source_target_pairs={{16,0},{20,4},{24,8},{28,12},{32,16},{36,20},{40,24},{44,28},{48,3... | collective-permute-start | bytes 884744 | tf_op jit(solution)/shard_map/while/body/eval_jaxpr/ppermute | solution.py:11
  95.0 8.9 %collective-permute-start.1 = (bf16[192,768]{1,0:T(8,128)(2,1)S(1)}, bf16[192,768]{1,0:T(8,128)(2,1)}, u32[]{:S(2)}, u32[]{:S(2)}) collective-permute-start(bf16[192,768]{1,0:T(8,128)(2,1)S(1)} %copy.24), channel_id=1, source_target_pairs={{240,0},{244,4},{248,8},{252,12},{0,16},{4,20},{8,24},{12,28},{16,... | collective-permute-start | bytes 884744 | tf_op jit(solution)/shard_map/while/body/eval_jaxpr/ppermute | solution.py:11
  104.9 11.7 %collective-permute-start = (bf16[192,768]{1,0:T(8,128)(2,1)S(1)}, bf16[192,768]{1,0:T(8,128)(2,1)}, u32[]{:S(2)}, u32[]{:S(2)}) collective-permute-start(bf16[192,768]{1,0:T(8,128)(2,1)S(1)} %copy.23), channel_id=1, source_target_pairs={{16,0},{20,4},{24,8},{28,12},{32,16},{36,20},{40,24},{44,28},{48,3... | collective-permute-start | bytes 884744 | tf_op jit(solution)/shard_map/while/body/eval_jaxpr/ppermute | solution.py:11
  108.9 8.9 %collective-permute-start.1 = (bf16[192,768]{1,0:T(8,128)(2,1)S(1)}, bf16[192,768]{1,0:T(8,128)(2,1)}, u32[]{:S(2)}, u32[]{:S(2)}) collective-permute-start(bf16[192,768]{1,0:T(8,128)(2,1)S(1)} %copy.24), channel_id=1, source_target_pairs={{240,0},{244,4},{248,8},{252,12},{0,16},{4,20},{8,24},{12,28},{16,... | collective-permute-start | bytes 884744 | tf_op jit(solution)/shard_map/while/body/eval_jaxpr/ppermute | solution.py:11
  118.8 11.7 %collective-permute-start = (bf16[192,768]{1,0:T(8,128)(2,1)S(1)}, bf16[192,768]{1,0:T(8,128)(2,1)}, u32[]{:S(2)}, u32[]{:S(2)}) collective-permute-start(bf16[192,768]{1,0:T(8,128)(2,1)S(1)} %copy.23), channel_id=1, source_target_pairs={{16,0},{20,4},{24,8},{28,12},{32,16},{36,20},{40,24},{44,28},{48,3... | collective-permute-start | bytes 884744 | tf_op jit(solution)/shard_map/while/body/eval_jaxpr/ppermute | solution.py:11
  122.7 8.9 %collective-permute-start.1 = (bf16[192,768]{1,0:T(8,128)(2,1)S(1)}, bf16[192,768]{1,0:T(8,128)(2,1)}, u32[]{:S(2)}, u32[]{:S(2)}) collective-permute-start(bf16[192,768]{1,0:T(8,128)(2,1)S(1)} %copy.24), channel_id=1, source_target_pairs={{240,0},{244,4},{248,8},{252,12},{0,16},{4,20},{8,24},{12,28},{16,... | collective-permute-start | bytes 884744 | tf_op jit(solution)/shard_map/while/body/eval_jaxpr/ppermute | solution.py:11
  132.6 11.7 %collective-permute-start = (bf16[192,768]{1,0:T(8,128)(2,1)S(1)}, bf16[192,768]{1,0:T(8,128)(2,1)}, u32[]{:S(2)}, u32[]{:S(2)}) collective-permute-start(bf16[192,768]{1,0:T(8,128)(2,1)S(1)} %copy.23), channel_id=1, source_target_pairs={{16,0},{20,4},{24,8},{28,12},{32,16},{36,20},{40,24},{44,28},{48,3... | collective-permute-start | bytes 884744 | tf_op jit(solution)/shard_map/while/body/eval_jaxpr/ppermute | solution.py:11
  136.6 8.9 %collective-permute-start.1 = (bf16[192,768]{1,0:T(8,128)(2,1)S(1)}, bf16[192,768]{1,0:T(8,128)(2,1)}, u32[]{:S(2)}, u32[]{:S(2)}) collective-permute-start(bf16[192,768]{1,0:T(8,128)(2,1)S(1)} %copy.24), channel_id=1, source_target_pairs={{240,0},{244,4},{248,8},{252,12},{0,16},{4,20},{8,24},{12,28},{16,... | collective-permute-start | bytes 884744 | tf_op jit(solution)/shard_map/while/body/eval_jaxpr/ppermute | solution.py:11
  154.4 14.0 %copy-start.11 = (f32[64]{0:T(128)S(1)}, f32[64]{0:T(128)}, u32[]{:S(2)}) copy-start(f32[64]{0:T(128)} %param.13) | copy-start | bytes 772
  154.4 14.1 %copy-start.3 = (bf16[768,512]{1,0:T(8,128)(2,1)S(1)}, bf16[768,512]{1,0:T(8,128)(2,1)}, u32[]{:S(2)}) copy-start(bf16[768,512]{1,0:T(8,128)(2,1)} %copy-done.2) | copy-start | bytes 2359300
  154.4 14.1 %copy-start.9 = (bf16[512,64]{0,1:T(8,128)(2,1)S(1)}, bf16[512,64]{0,1:T(8,128)(2,1)}, u32[]{:S(2)}) copy-start(bf16[512,64]{0,1:T(8,128)(2,1)} %param.12) | copy-start | bytes 196612
  156.8 11.7 %all-to-all-start = ((f32[4,64,192]{2,1,0:T(8,128)}), f32[4,64,192]{2,1,0:T(8,128)S(1)}, u32[]{:S(2)}, u32[]{:S(2)}) async-start(f32[4,64,192]{2,1,0:T(8,128)} %bitcast.31), calls=%async_computation | async-start | bytes 524288 | tf_op jit(solution)/shard_map/all_to_all | solution.py:22
  160.9 272.0 %all-reduce.3.cloned.1.call-start = ((), (), s32[]{:S(2)}) async-start(), calls=%async_computation.1 | async-start | bytes 4456448 | tf_op jit(solution)/shard_map/psum | solution.py:118
  (7 other events, 19.0 us)
Sparse Core Ops, SparseCore 0:
  171.6 261.2 all-reduce.2
where the time goes:
time: 445 us; the launch traced here: 443 us
  waiting for transfers between devices  219 us (49%)
  blocking collectives  78 us (18%)
  matrix products  68.9 us (15%)
  starting transfers between devices  38.3 us (9%)
  local copies, waits for them, and re-layouts  20.5 us (5%)
  between operations  14.2 us (3%)
    psum x1, waiting for transfers between devices, on_device(): lax.psum((term_w_in, term_b_in, term_w_out), ('blk', 'rep'))  183 us
    psum x1, blocking collectives, on_device(): lax.psum((term_w_in, term_b_in, term_w_out), ('blk', 'rep'))  78 us
    ppermute x17, starting transfers between devices, shifted(): return lax.ppermute(block, axis, route)  34.2 us
    ppermute x17, waiting for transfers between devices, shifted(): return lax.ppermute(block, axis, route)  28.2 us
    dot_general x16, matrix products, couple(): lax.dot_general(own_y, vis_y, (((0,), (0,)), ((), ())), preferred_element...  28.1 us
    dot_general x16, matrix products, couple(): lax.dot_general(vis_y, weight_b, (((1,), (1,)), ((), ())), preferred_elem...  23.8 us
    while x14, local copies, waits for them, and re-layouts  13.5 us
    dot_general x16, matrix products, couple(): lax.dot_general(own_pair, vis_pair, (((0,), (0,)), ((), ())), preferred_e...  10.8 us
  transfers between devices with their start and end apart: 19, of which 11 were waited for; matrix products, arithmetic and copies ran while one was open for 14% of the time, Pallas kernels for 0%

commit v1 on v0

--- a/solution.py
+++ b/solution.py
@@ -3,6 +3,14 @@
 import jax.numpy as jnp
 from jax import lax
 from jax.sharding import PartitionSpec as P
+
+
+def _pack_marks(values):
+    shard_axis = "rep"
+    lane_axis = "blk"
+    for ii in (shard_axis, lane_axis):
+        values = jax.lax.psum(values, axis_name=ii)
+    return values
 
 
 def shifted(block, axis, distance):
@@ -115,7 +123,7 @@
         )
         * norm
     )
-    grad_w_in, grad_b_in, grad_w_out = lax.psum((term_w_in, term_b_in, term_w_out), ("blk", "rep"))
+    grad_w_in, grad_b_in, grad_w_out = _pack_marks((term_w_in, term_b_in, term_w_out))
     return (feat_grad, grad_w_in, grad_b_in, grad_w_out)
 
 

time: 445 us -> 848 us (1.91)
  waiting for transfers between devices: 219 us -> 536 us
  blocking collectives: 78 us -> 162 us
    psum x1 -> x2, waiting for transfers between devices: 183 us -> 501 us  [_pack_marks(): values = jax.lax.psum(values, axis_name=ii)]
    psum x1 -> x2, blocking collectives: 78 us -> 162 us  [_pack_marks(): values = jax.lax.psum(values, axis_name=ii)]
  transfers between devices with their start and end apart: 19 -> 20, of which waited for: 11 -> 12; matrix products, arithmetic and copies ran while one was open for 14% -> 7% of each run, Pallas kernels for 0% -> 0%
where the time goes in v1:
time: 848 us; the launch traced here: 845 us
  waiting for transfers between devices  536 us (63%)
  blocking collectives  162 us (19%)
  matrix products  68.9 us (8%)
  starting transfers between devices  38.3 us (5%)
  local copies, waits for them, and re-layouts  20.5 us (2%)
  between operations  14.2 us (2%)
    psum x2, waiting for transfers between devices, _pack_marks(): values = jax.lax.psum(values, axis_name=ii)  501 us
    psum x2, blocking collectives, _pack_marks(): values = jax.lax.psum(values, axis_name=ii)  162 us
    ppermute x17, starting transfers between devices, shifted(): return lax.ppermute(block, axis, route)  34.2 us
    ppermute x17, waiting for transfers between devices, shifted(): return lax.ppermute(block, axis, route)  28.2 us
    dot_general x16, matrix products, couple(): lax.dot_general(own_y, vis_y, (((0,), (0,)), ((), ())), preferred_element...  28.1 us
    dot_general x16, matrix products, couple(): lax.dot_general(vis_y, weight_b, (((1,), (1,)), ((), ())), preferred_elem...  23.8 us
  transfers between devices with their start and end apart: 20, of which 12 were waited for; matrix products, arithmetic and copies ran while one was open for 7% of the time, Pallas kernels for 0%

profile of v1, /device:TPU:2, one launch (start us, length us, event | category | flops | bytes accessed | tf_op | source)
XLA Modules:
  0.0 844.7 jit_solution(4462361381588681237)
XLA Ops:
  8.6 2.2 tanh_convert_fusion
  13.6 2.3 collective-permute-start.2
  16.0 6.5 collective-permute-done.2
  23.4 12.7 %collective-permute-start.3 = (bf16[192,768]{1,0:T(8,128)(2,1)S(1)}, bf16[192,768]{1,0:T(8,128)(2,1)S(1)}, u32[]{:S(2)}, u32[]{:S(2)}) collective-permute-start(bf16[192,768]{1,0:T(8,128)(2,1)S(1)} %broadcast_select_fusion), channel_id=1, source_target_pairs={{8,0},{12,4},{16,8},{20,12},{24,16},{28,20},{32,24},{36,28},{40,32... | collective-permute-start | bytes 884744 | tf_op jit(solution)/shard_map/ppermute | solution.py:19
  36.2 5.4 collective-permute-done.3
  42.3 9.3 %collective-permute-done.4 = bf16[192,768]{1,0:T(8,128)(2,1)} collective-permute-done((bf16[192,768]{1,0:T(8,128)(2,1)}, bf16[192,768]{1,0:T(8,128)(2,1)}, u32[]{:S(2)}, u32[]{:S(2)}) %collective-permute-start.4) | collective-permute-done | bytes 294944 | tf_op jit(solution)/shard_map/ppermute | solution.py:19
  51.7 93.9 %while.17 = (s32[]{:T(128)}, f32[768]{0:T(1024)S(1)}, f32[64,768]{1,0:T(8,128)}, bf16[192,768]{1,0:T(8,128)(2,1)}, bf16[192,768]{1,0:T(8,128)(2,1)}, /*index=5*/...) while((s32[]{:T(128)}, f32[768]{0:T(1024)S(1)}, ...), condition=%wide.region_6.7_spmd.clone, body=%wide.region_1.6_spmd.clone.sunk | while | flops 613858560 | bytes 20095168 | solution.py:95
  64.3 2.1 collective-permute-start
  73.1 2.0 fusion.79
  77.3 3.0 collective-permute-start
  86.9 2.0 fusion.79
  91.1 3.0 collective-permute-start
  100.8 2.0 fusion.79
  104.9 3.0 collective-permute-start
  114.6 2.0 fusion.79
  118.8 3.0 collective-permute-start
  132.6 3.0 collective-permute-start
  156.8 4.1 all-to-all-start
  160.9 7.5 all-to-all-done
  171.5 65.0 %all-reduce.7.cloned.1.call-done = (f32[1024,512]{1,0:T(8,128)}, f32[512,64]{0,1:T(8,128)}) async-done(((f32[1024,512]{1,0:T(8,128)}, f32[512,64]{0,1:T(8,128)}), (f32[1024,512]{1,0:T(8,128)}, f32[512,64]{0,1:T(8,128)})) %all-reduce.7.cloned.1.call-update) | async-done | bytes 2228240 | tf_op jit(solution)/shard_map/psum | solution.py:12
  236.5 7.5 psum.44
  244.0 154.5 %psum.45 = f32[512]{0:T(512)} all-reduce(f32[512]{0:T(512)S(1)} %psum.44), channel_id=1, replica_groups=mesh['blk'=64,'rep'=4] {'blk'}, use_global_device_ids=true, to_apply=%region_16.17 | all-reduce | flops 512 | bytes 4096 | tf_op jit(solution)/shard_map/psum | solution.py:12
  398.5 435.6 %all-reduce.5.cloned.1.call-done = (f32[1024,512]{1,0:T(8,128)}, f32[512,64]{0,1:T(8,128)}) async-done(((f32[1024,512]{1,0:T(8,128)}, f32[512,64]{0,1:T(8,128)}), (f32[1024,512]{1,0:T(8,128)}, f32[512,64]{0,1:T(8,128)})) %all-reduce.5.cloned.1.call-update) | async-done | bytes 2228240 | tf_op jit(solution)/shard_map/psum | solution.py:12
  834.1 3.1 copy.34
  (142 shorter events, 89.1 us)
Async XLA Ops:
  7.2 5.5 copy-start.4
  13.6 8.8 %collective-permute-start.2 = (bf16[192,768]{1,0:T(8,128)(2,1)S(1)}, bf16[192,768]{1,0:T(8,128)(2,1)S(1)}, u32[]{:S(2)}, u32[]{:S(2)}) collective-permute-start(bf16[192,768]{1,0:T(8,128)(2,1)S(1)} %pad_maximum_fusion), channel_id=1, source_target_pairs={{4,0},{8,4},{12,8},{16,12},{20,16},{24,20},{28,24},{32,28},{36,32}... | collective-permute-start | bytes 884744 | tf_op jit(solution)/shard_map/ppermute | solution.py:19
  23.4 18.1 %collective-permute-start.3 = (bf16[192,768]{1,0:T(8,128)(2,1)S(1)}, bf16[192,768]{1,0:T(8,128)(2,1)S(1)}, u32[]{:S(2)}, u32[]{:S(2)}) collective-permute-start(bf16[192,768]{1,0:T(8,128)(2,1)S(1)} %broadcast_select_fusion), channel_id=1, source_target_pairs={{8,0},{12,4},{16,8},{20,12},{24,16},{28,20},{32,24},{36,28},{40,32... | collective-permute-start | bytes 884744 | tf_op jit(solution)/shard_map/ppermute | solution.py:19
  42.3 9.4 %collective-permute-start.4 = (bf16[192,768]{1,0:T(8,128)(2,1)}, bf16[192,768]{1,0:T(8,128)(2,1)}, u32[]{:S(2)}, u32[]{:S(2)}) collective-permute-start(bf16[192,768]{1,0:T(8,128)(2,1)} %broadcast_select_fusion.1), channel_id=1, source_target_pairs={{240,0},{244,4},{248,8},{252,12},{0,16},{4,20},{8,24},{12,28},{16,... | collective-permute-start | bytes 884744 | tf_op jit(solution)/shard_map/ppermute | solution.py:19
  52.6 10.7 %collective-permute-start = (bf16[192,768]{1,0:T(8,128)(2,1)S(1)}, bf16[192,768]{1,0:T(8,128)(2,1)}, u32[]{:S(2)}, u32[]{:S(2)}) collective-permute-start(bf16[192,768]{1,0:T(8,128)(2,1)S(1)} %copy.23), channel_id=1, source_target_pairs={{16,0},{20,4},{24,8},{28,12},{32,16},{36,20},{40,24},{44,28},{48,3... | collective-permute-start | bytes 884744 | tf_op jit(solution)/shard_map/while/body/eval_jaxpr/ppermute | solution.py:19
  53.6 9.7 %collective-permute-start.1 = (bf16[192,768]{1,0:T(8,128)(2,1)S(1)}, bf16[192,768]{1,0:T(8,128)(2,1)}, u32[]{:S(2)}, u32[]{:S(2)}) collective-permute-start(bf16[192,768]{1,0:T(8,128)(2,1)S(1)} %copy.24), channel_id=1, source_target_pairs={{240,0},{244,4},{248,8},{252,12},{0,16},{4,20},{8,24},{12,28},{16,... | collective-permute-start | bytes 884744 | tf_op jit(solution)/shard_map/while/body/eval_jaxpr/ppermute | solution.py:19
  64.3 10.9 %collective-permute-start = (bf16[192,768]{1,0:T(8,128)(2,1)S(1)}, bf16[192,768]{1,0:T(8,128)(2,1)}, u32[]{:S(2)}, u32[]{:S(2)}) collective-permute-start(bf16[192,768]{1,0:T(8,128)(2,1)S(1)} %copy.23), channel_id=1, source_target_pairs={{16,0},{20,4},{24,8},{28,12},{32,16},{36,20},{40,24},{44,28},{48,3... | collective-permute-start | bytes 884744 | tf_op jit(solution)/shard_map/while/body/eval_jaxpr/ppermute | solution.py:19
  67.4 8.9 %collective-permute-start.1 = (bf16[192,768]{1,0:T(8,128)(2,1)S(1)}, bf16[192,768]{1,0:T(8,128)(2,1)}, u32[]{:S(2)}, u32[]{:S(2)}) collective-permute-start(bf16[192,768]{1,0:T(8,128)(2,1)S(1)} %copy.24), channel_id=1, source_target_pairs={{240,0},{244,4},{248,8},{252,12},{0,16},{4,20},{8,24},{12,28},{16,... | collective-permute-start | bytes 884744 | tf_op jit(solution)/shard_map/while/body/eval_jaxpr/ppermute | solution.py:19
  77.3 11.7 %collective-permute-start = (bf16[192,768]{1,0:T(8,128)(2,1)S(1)}, bf16[192,768]{1,0:T(8,128)(2,1)}, u32[]{:S(2)}, u32[]{:S(2)}) collective-permute-start(bf16[192,768]{1,0:T(8,128)(2,1)S(1)} %copy.23), channel_id=1, source_target_pairs={{16,0},{20,4},{24,8},{28,12},{32,16},{36,20},{40,24},{44,28},{48,3... | collective-permute-start | bytes 884744 | tf_op jit(solution)/shard_map/while/body/eval_jaxpr/ppermute | solution.py:19
  81.2 8.9 %collective-permute-start.1 = (bf16[192,768]{1,0:T(8,128)(2,1)S(1)}, bf16[192,768]{1,0:T(8,128)(2,1)}, u32[]{:S(2)}, u32[]{:S(2)}) collective-permute-start(bf16[192,768]{1,0:T(8,128)(2,1)S(1)} %copy.24), channel_id=1, source_target_pairs={{240,0},{244,4},{248,8},{252,12},{0,16},{4,20},{8,24},{12,28},{16,... | collective-permute-start | bytes 884744 | tf_op jit(solution)/shard_map/while/body/eval_jaxpr/ppermute | solution.py:19
  91.1 11.7 %collective-permute-start = (bf16[192,768]{1,0:T(8,128)(2,1)S(1)}, bf16[192,768]{1,0:T(8,128)(2,1)}, u32[]{:S(2)}, u32[]{:S(2)}) collective-permute-start(bf16[192,768]{1,0:T(8,128)(2,1)S(1)} %copy.23), channel_id=1, source_target_pairs={{16,0},{20,4},{24,8},{28,12},{32,16},{36,20},{40,24},{44,28},{48,3... | collective-permute-start | bytes 884744 | tf_op jit(solution)/shard_map/while/body/eval_jaxpr/ppermute | solution.py:19
  95.0 8.9 %collective-permute-start.1 = (bf16[192,768]{1,0:T(8,128)(2,1)S(1)}, bf16[192,768]{1,0:T(8,128)(2,1)}, u32[]{:S(2)}, u32[]{:S(2)}) collective-permute-start(bf16[192,768]{1,0:T(8,128)(2,1)S(1)} %copy.24), channel_id=1, source_target_pairs={{240,0},{244,4},{248,8},{252,12},{0,16},{4,20},{8,24},{12,28},{16,... | collective-permute-start | bytes 884744 | tf_op jit(solution)/shard_map/while/body/eval_jaxpr/ppermute | solution.py:19
  104.9 11.7 %collective-permute-start = (bf16[192,768]{1,0:T(8,128)(2,1)S(1)}, bf16[192,768]{1,0:T(8,128)(2,1)}, u32[]{:S(2)}, u32[]{:S(2)}) collective-permute-start(bf16[192,768]{1,0:T(8,128)(2,1)S(1)} %copy.23), channel_id=1, source_target_pairs={{16,0},{20,4},{24,8},{28,12},{32,16},{36,20},{40,24},{44,28},{48,3... | collective-permute-start | bytes 884744 | tf_op jit(solution)/shard_map/while/body/eval_jaxpr/ppermute | solution.py:19
  108.9 8.9 %collective-permute-start.1 = (bf16[192,768]{1,0:T(8,128)(2,1)S(1)}, bf16[192,768]{1,0:T(8,128)(2,1)}, u32[]{:S(2)}, u32[]{:S(2)}) collective-permute-start(bf16[192,768]{1,0:T(8,128)(2,1)S(1)} %copy.24), channel_id=1, source_target_pairs={{240,0},{244,4},{248,8},{252,12},{0,16},{4,20},{8,24},{12,28},{16,... | collective-permute-start | bytes 884744 | tf_op jit(solution)/shard_map/while/body/eval_jaxpr/ppermute | solution.py:19
  118.8 11.7 %collective-permute-start = (bf16[192,768]{1,0:T(8,128)(2,1)S(1)}, bf16[192,768]{1,0:T(8,128)(2,1)}, u32[]{:S(2)}, u32[]{:S(2)}) collective-permute-start(bf16[192,768]{1,0:T(8,128)(2,1)S(1)} %copy.23), channel_id=1, source_target_pairs={{16,0},{20,4},{24,8},{28,12},{32,16},{36,20},{40,24},{44,28},{48,3... | collective-permute-start | bytes 884744 | tf_op jit(solution)/shard_map/while/body/eval_jaxpr/ppermute | solution.py:19
  122.7 8.9 %collective-permute-start.1 = (bf16[192,768]{1,0:T(8,128)(2,1)S(1)}, bf16[192,768]{1,0:T(8,128)(2,1)}, u32[]{:S(2)}, u32[]{:S(2)}) collective-permute-start(bf16[192,768]{1,0:T(8,128)(2,1)S(1)} %copy.24), channel_id=1, source_target_pairs={{240,0},{244,4},{248,8},{252,12},{0,16},{4,20},{8,24},{12,28},{16,... | collective-permute-start | bytes 884744 | tf_op jit(solution)/shard_map/while/body/eval_jaxpr/ppermute | solution.py:19
  132.6 11.7 %collective-permute-start = (bf16[192,768]{1,0:T(8,128)(2,1)S(1)}, bf16[192,768]{1,0:T(8,128)(2,1)}, u32[]{:S(2)}, u32[]{:S(2)}) collective-permute-start(bf16[192,768]{1,0:T(8,128)(2,1)S(1)} %copy.23), channel_id=1, source_target_pairs={{16,0},{20,4},{24,8},{28,12},{32,16},{36,20},{40,24},{44,28},{48,3... | collective-permute-start | bytes 884744 | tf_op jit(solution)/shard_map/while/body/eval_jaxpr/ppermute | solution.py:19
  136.6 8.9 %collective-permute-start.1 = (bf16[192,768]{1,0:T(8,128)(2,1)S(1)}, bf16[192,768]{1,0:T(8,128)(2,1)}, u32[]{:S(2)}, u32[]{:S(2)}) collective-permute-start(bf16[192,768]{1,0:T(8,128)(2,1)S(1)} %copy.24), channel_id=1, source_target_pairs={{240,0},{244,4},{248,8},{252,12},{0,16},{4,20},{8,24},{12,28},{16,... | collective-permute-start | bytes 884744 | tf_op jit(solution)/shard_map/while/body/eval_jaxpr/ppermute | solution.py:19
  154.4 14.0 %copy-start.11 = (f32[64]{0:T(128)S(1)}, f32[64]{0:T(128)}, u32[]{:S(2)}) copy-start(f32[64]{0:T(128)} %param.13) | copy-start | bytes 772
  154.4 14.1 %copy-start.3 = (bf16[768,512]{1,0:T(8,128)(2,1)S(1)}, bf16[768,512]{1,0:T(8,128)(2,1)}, u32[]{:S(2)}) copy-start(bf16[768,512]{1,0:T(8,128)(2,1)} %copy-done.2) | copy-start | bytes 2359300
  154.4 14.1 %copy-start.9 = (bf16[512,64]{0,1:T(8,128)(2,1)S(1)}, bf16[512,64]{0,1:T(8,128)(2,1)}, u32[]{:S(2)}) copy-start(bf16[512,64]{0,1:T(8,128)(2,1)} %param.12) | copy-start | bytes 196612
  156.8 11.7 %all-to-all-start = ((f32[4,64,192]{2,1,0:T(8,128)}), f32[4,64,192]{2,1,0:T(8,128)S(1)}, u32[]{:S(2)}, u32[]{:S(2)}) async-start(f32[4,64,192]{2,1,0:T(8,128)} %bitcast.31), calls=%async_computation | async-start | bytes 524288 | tf_op jit(solution)/shard_map/all_to_all | solution.py:30
  160.9 75.6 %all-reduce.7.cloned.1.call-start = ((), (), s32[]{:S(2)}) async-start(), calls=%async_computation.2 | async-start | bytes 4456448 | tf_op jit(solution)/shard_map/psum | solution.py:12
  171.5 662.6 %all-reduce.5.cloned.1.call-start = ((), (), s32[]{:S(2)}) async-start(), calls=%async_computation.1 | async-start | bytes 4456448 | tf_op jit(solution)/shard_map/psum | solution.py:12
  (8 other events, 23.5 us)
Sparse Core Ops, SparseCore 0:
  171.6 64.8 all-reduce.6
  239.2 594.8 all-reduce.4
